TPU v7x, 32 devices: a whole 2x2x4 slice. The times are simulated.
32 devices in a mesh: pix: 8 (over y, x, core), chan: 4 (over z).
Axes of the slice: x: 2, y: 2, z: 4, core: 2. Of those that a mesh axis runs over, the one named last changes fastest.
Arguments:
- sky_map: bfloat16 [2048, 4096], P('pix', 'chan'), may hold values from -6 to 6
- channel_flags: int32 [4096], P('chan'), may hold values 0 or 1
- ripple_modes: int32 [4096], replicated, may hold values 0 or 1
- galaxy_block: int32 [128], P('pix'), may hold values from 0 to 127
- galaxy_offset: int32 [128], P('pix'), may hold values from 0 to 3968
- galaxy_weight: bfloat16 [128, 16, 128], P('pix'), may hold values from 0.099609375 to 10
Outputs:
- filtered: bfloat16 [2048, 4096], P(('pix', 'chan'))
- stack: float32 [16, 128], replicated
All inputs are finite; a program needn't handle non-finite values. No bound on the sum of `channel_flags` on one device may be relied on, other than what follows from the above.
Results may differ from a plain program's by a relative error of at most 0.0051.
Values may be sent and summed in bfloat16 or wider, within the bound.
A program may use at most 128 MiB of HBM per device.

v0:
```python
import jax
import jax.numpy as jnp
from jax import lax
from jax.sharding import PartitionSpec as P


def basis_columns(total, start, count):
    rows = jnp.arange(total, dtype=jnp.int32)[:, None]
    cols = start + jnp.arange(count, dtype=jnp.int32)[None, :]
    half = total // 2
    is_cos = cols <= half
    mode = jnp.where(is_cos, cols, cols - half)
    phase = rows * mode % total
    angle = phase.astype(jnp.float32) * (2.0 * 3.141592653589793 / total)
    edge = jnp.logical_or(cols == 0, cols == half)
    factor = jnp.where(edge, (1.0 / total) ** 0.5, (2.0 / total) ** 0.5).astype(jnp.float32)
    value = jnp.where(is_cos, jnp.cos(angle), jnp.sin(angle)) * factor
    return value.astype(jnp.bfloat16)


def filter_lines(lines, ripple_modes):
    total = lines.shape[1]
    width = min(512, total)
    ripple = jnp.zeros(lines.shape, jnp.float32)
    for start in range(0, total, width):
        table = basis_columns(total, start, width)
        coeffs = jnp.dot(lines, table, preferred_element_type=jnp.float32)
        chosen = ripple_modes[start : start + width].astype(jnp.float32)
        kept = (coeffs * chosen[None, :]).astype(jnp.bfloat16)
        ripple = ripple + lax.dot_general(
            kept, table, (((1,), (1,)), ((), ())), preferred_element_type=jnp.float32
        )
    return (lines.astype(jnp.float32) - ripple).astype(jnp.bfloat16)


def owned_panels(cube, blocks, offsets, first_block, width):
    count = cube.shape[0]
    local = blocks - first_block
    owned = jnp.logical_and(local >= 0, local < count)
    safe = jnp.clip(local, 0, count - 1).astype(jnp.int32)
    patch = cube.shape[1]

    def take(block, offset):
        zero = jnp.zeros((), jnp.int32)
        return lax.dynamic_slice(cube, (block, zero, offset.astype(jnp.int32)), (1, patch, width))[
            0
        ]

    panels = jax.vmap(take)(safe, offsets).astype(jnp.float32)
    return jnp.where(owned[:, None, None], panels, 0.0)


def body(sky_map, channel_flags, ripple_modes, galaxy_block, galaxy_offset, galaxy_weight):
    groups = lax.axis_size("chan")
    flagged = sky_map * channel_flags.astype(jnp.bfloat16)[None, :]
    rows_here = flagged.shape[0] // groups
    arranged = flagged.reshape(groups, rows_here, flagged.shape[1])
    regrouped = lax.all_to_all(arranged, "chan", split_axis=0, concat_axis=2, tiled=True)
    lines = regrouped.reshape(rows_here, regrouped.shape[2])
    filtered = filter_lines(lines, ripple_modes)
    patch = galaxy_weight.shape[1]
    width = galaxy_weight.shape[2]
    cube = filtered.reshape(rows_here // patch, patch, filtered.shape[1])
    device = lax.axis_index("pix") * groups + lax.axis_index("chan")
    first_block = device * (rows_here // patch)
    blocks = lax.all_gather(galaxy_block, "pix", axis=0, tiled=True)
    offsets = lax.all_gather(galaxy_offset, "pix", axis=0, tiled=True)
    weights = lax.all_gather(galaxy_weight, "pix", axis=0, tiled=True)
    panels = owned_panels(cube, blocks, offsets, first_block, width)
    weight_f = weights.astype(jnp.float32)
    numerator = jnp.sum(weight_f * panels, axis=0)
    power = jnp.sum(weight_f * weight_f, axis=0)
    numerator, power = (numerator, power)
    numerator = lax.psum(numerator, ("pix", "chan"))
    return (filtered, numerator / jnp.sqrt(power))


def solution(mesh):
    in_specs = (P("pix", "chan"), P("chan"), P(), P("pix"), P("pix"), P("pix", None, None))
    out_specs = (P(("pix", "chan"), None), P())
    return jax.shard_map(body, mesh=mesh, in_specs=in_specs, out_specs=out_specs, check_vma=False)
```

profile of v0, /device:TPU:0, one launch (start us, length us, event | category | flops | bytes accessed | tf_op | source)
XLA Modules:
  0.0 682.4 jit_solution(11037122949243783800)
XLA Ops:
  0.6 0.7 convert_element_type.146
  1.3 1.9 broadcast_multiply_fusion
  3.2 6.3 all-to-all-start
  9.8 0.6 fusion.122
  10.4 0.6 fusion.87
  11.5 1.3 copy.12
  12.7 1.2 dynamic-slice
  14.6 0.9 dynamic-update-slice
  15.5 0.8 dynamic-update-slice.1
  16.3 8.0 %all-reduce.2 = (s32[128]{0:T(128)S(1)}, s32[128]{0:T(128)S(1)}) all-reduce(s32[128]{0:T(128)S(1)} %dynamic-update-slice.1, s32[128]{0:T(128)S(1)} %dynamic-update-slice), channel_id=1, replica_groups=mesh['pix'=8,'chan'=4] {'pix'}, use_global_device_ids=true, to_apply=%add.1 | all-reduce | flops 256 | bytes 2048
  24.3 39.1 %all_gather.9 = bf16[128,16,128]{1,0,2:T(8,128)(2,1)} all-gather(bf16[16,16,128]{1,0,2:T(8,128)(2,1)S(1)} %copy.12), channel_id=1, replica_groups=mesh['pix'=8,'chan'=4] {'pix'}, dimensions={0}, use_global_device_ids=true | all-gather | bytes 589824 | tf_op jit(solution)/shard_map/all_gather | solution.py:68
  65.8 34.2 %fusion.76.clone.5 = bf16[64,512]{1,0:T(8,128)(2,1)S(1)} fusion(bf16[64,4096]{1,0:T(8,128)(2,1)S(1)} %bitcast.45, f32[512]{0:T(512)S(1)} %fusion.124, s32[512]{0:T(512)S(1)} %get-tuple-element.16, pred[512]{0:T(512)(128)(4,1)S(1)} %iota_compare_fusion.2, f32[512]{0:T(512)S(1)} %get-tuple-element.14), kind=kOutput, calls=%fused_computation.119.clone.clone.clone.2 | convolution fusion | flops 304152576 | bytes 596480 | tf_op jit(solution)/shard_map/dot_general | solution.py:27
  100.0 34.1 %fusion.59 = f32[64,4096]{1,0:T(8,128)S(1)} fusion(f32[512]{0:T(512)S(1)} %fusion.124, s32[512]{0:T(512)S(1)} %get-tuple-element.16, pred[512]{0:T(512)(128)(4,1)S(1)} %iota_compare_fusion.2, bf16[64,512]{1,0:T(8,128)(2,1)S(1)} %fusion.76.clone.5), kind=kOutput, calls=%fused_computation.102 | convolution fusion | flops 304087040 | bytes 1118720 | tf_op jit(solution)/shard_map/dot_general | solution.py:30
  134.1 34.2 %fusion.75.clone.2 = bf16[64,512]{1,0:T(8,128)(2,1)S(1)} fusion(bf16[64,4096]{1,0:T(8,128)(2,1)S(1)} %bitcast.46, f32[512]{0:T(512)S(1)} %fusion.110, s32[512]{0:T(512)S(1)} %add_select_fusion.11, pred[512]{0:T(512)(128)(4,1)S(1)} %fusion.108, f32[512]{0:T(512)S(1)} %get-tuple-element.13), kind=kOutput, calls=%fused_computation.118.clone.clone.clone | convolution fusion | flops 304152576 | bytes 596480 | tf_op jit(solution)/shard_map/dot_general | solution.py:27
  168.3 34.1 %convolution_add_fusion.6 = f32[64,4096]{1,0:T(8,128)S(1)} fusion(f32[64,4096]{1,0:T(8,128)S(1)} %fusion.59, f32[512]{0:T(512)S(1)} %fusion.110, s32[512]{0:T(512)S(1)} %add_select_fusion.11, pred[512]{0:T(512)(128)(4,1)S(1)} %fusion.108, bf16[64,512]{1,0:T(8,128)(2,1)S(1)} %fusion.75.clone.2), kind=kOutput, calls=%fused_computation.93 | convolution fusion | flops 304349184 | bytes 2167296 | tf_op jit(solution)/shard_map/dot_general | solution.py:30
  202.4 34.2 %fusion.74.clone.2 = bf16[64,512]{1,0:T(8,128)(2,1)S(1)} fusion(bf16[64,4096]{1,0:T(8,128)(2,1)S(1)} %bitcast.47, f32[512]{0:T(512)S(1)} %fusion.112, s32[512]{0:T(512)S(1)} %add_select_fusion.10, pred[512]{0:T(512)(128)(4,1)S(1)} %fusion.105, f32[512]{0:T(512)S(1)} %get-tuple-element.12), kind=kOutput, calls=%fused_computation.117.clone.clone.clone | convolution fusion | flops 304152576 | bytes 596480 | tf_op jit(solution)/shard_map/dot_general | solution.py:27
  236.7 34.1 %convolution_add_fusion.5 = f32[64,4096]{1,0:T(8,128)S(1)} fusion(f32[64,4096]{1,0:T(8,128)S(1)} %convolution_add_fusion.6, f32[512]{0:T(512)S(1)} %fusion.112, s32[512]{0:T(512)S(1)} %add_select_fusion.10, pred[512]{0:T(512)(128)(4,1)S(1)} %fusion.105, bf16[64,512]{1,0:T(8,128)(2,1)S(1)} %fusion.74.clone.2), kind=kOutput, calls=%fused_computation.92 | convolution fusion | flops 304349184 | bytes 2167296 | tf_op jit(solution)/shard_map/dot_general | solution.py:30
  270.7 34.2 %fusion.73.clone.2 = bf16[64,512]{1,0:T(8,128)(2,1)S(1)} fusion(bf16[64,4096]{1,0:T(8,128)(2,1)S(1)} %bitcast.48, f32[512]{0:T(512)S(1)} %fusion.114, s32[512]{0:T(512)S(1)} %add_select_fusion.9, pred[512]{0:T(512)(128)(4,1)S(1)} %fusion.102, f32[512]{0:T(512)S(1)} %get-tuple-element.11), kind=kOutput, calls=%fused_computation.116.clone.clone.clone | convolution fusion | flops 304152576 | bytes 596480 | tf_op jit(solution)/shard_map/dot_general | solution.py:27
  305.0 34.1 %convolution_add_fusion.4 = f32[64,4096]{1,0:T(8,128)S(1)} fusion(f32[64,4096]{1,0:T(8,128)S(1)} %convolution_add_fusion.5, f32[512]{0:T(512)S(1)} %fusion.114, s32[512]{0:T(512)S(1)} %add_select_fusion.9, pred[512]{0:T(512)(128)(4,1)S(1)} %fusion.102, bf16[64,512]{1,0:T(8,128)(2,1)S(1)} %fusion.73.clone.2), kind=kOutput, calls=%fused_computation.91 | convolution fusion | flops 304349184 | bytes 2167296 | tf_op jit(solution)/shard_map/dot_general | solution.py:30
  339.1 34.2 %fusion.72.clone.2 = bf16[64,512]{1,0:T(8,128)(2,1)S(1)} fusion(bf16[64,4096]{1,0:T(8,128)(2,1)S(1)} %bitcast.49, f32[512]{0:T(512)S(1)} %fusion.116, s32[512]{0:T(512)S(1)} %iota_select_fusion, pred[512]{0:T(512)(128)(4,1)S(1)} %fusion.99, f32[512]{0:T(512)S(1)} %get-tuple-element.10), kind=kOutput, calls=%fused_computation.115.clone.clone.clone | convolution fusion | flops 304152576 | bytes 596480 | tf_op jit(solution)/shard_map/dot_general | solution.py:27
  373.3 34.1 %convolution_add_fusion.3 = f32[64,4096]{1,0:T(8,128)S(1)} fusion(f32[64,4096]{1,0:T(8,128)S(1)} %convolution_add_fusion.4, f32[512]{0:T(512)S(1)} %fusion.116, s32[512]{0:T(512)S(1)} %iota_select_fusion, pred[512]{0:T(512)(128)(4,1)S(1)} %fusion.99, bf16[64,512]{1,0:T(8,128)(2,1)S(1)} %fusion.72.clone.2), kind=kOutput, calls=%fused_computation.90 | convolution fusion | flops 304349184 | bytes 2167296 | tf_op jit(solution)/shard_map/dot_general | solution.py:30
  407.4 34.2 %fusion.71.clone.2 = bf16[64,512]{1,0:T(8,128)(2,1)S(1)} fusion(bf16[64,4096]{1,0:T(8,128)(2,1)S(1)} %bitcast.50, f32[512]{0:T(512)S(1)} %fusion.118, s32[512]{0:T(512)S(1)} %fusion.95, pred[512]{0:T(512)(128)(4,1)S(1)} %fusion.96, f32[512]{0:T(512)S(1)} %get-tuple-element.9), kind=kOutput, calls=%fused_computation.114.clone.clone.clone | convolution fusion | flops 304152576 | bytes 596480 | tf_op jit(solution)/shard_map/dot_general | solution.py:27
  441.7 34.1 %convolution_add_fusion.2 = f32[64,4096]{1,0:T(8,128)S(1)} fusion(f32[64,4096]{1,0:T(8,128)S(1)} %convolution_add_fusion.3, f32[512]{0:T(512)S(1)} %fusion.118, s32[512]{0:T(512)S(1)} %fusion.95, pred[512]{0:T(512)(128)(4,1)S(1)} %fusion.96, bf16[64,512]{1,0:T(8,128)(2,1)S(1)} %fusion.71.clone.2), kind=kOutput, calls=%fused_computation.89 | convolution fusion | flops 304349184 | bytes 2167296 | tf_op jit(solution)/shard_map/dot_general | solution.py:30
  475.8 34.2 %fusion.70.clone.5 = bf16[64,512]{1,0:T(8,128)(2,1)S(1)} fusion(bf16[64,4096]{1,0:T(8,128)(2,1)S(1)} %bitcast.51, f32[512]{0:T(512)S(1)} %fusion.120, s32[512]{0:T(512)S(1)} %fusion.91, pred[512]{0:T(512)(128)(4,1)S(1)} %fusion.92, f32[512]{0:T(512)S(1)} %get-tuple-element.15), kind=kOutput, calls=%fused_computation.113.clone.clone.clone.2 | convolution fusion | flops 304152576 | bytes 596480 | tf_op jit(solution)/shard_map/dot_general | solution.py:27
  510.0 34.1 %convolution_add_fusion.1 = f32[64,4096]{1,0:T(8,128)S(1)} fusion(f32[64,4096]{1,0:T(8,128)S(1)} %convolution_add_fusion.2, f32[512]{0:T(512)S(1)} %fusion.120, s32[512]{0:T(512)S(1)} %fusion.91, pred[512]{0:T(512)(128)(4,1)S(1)} %fusion.92, bf16[64,512]{1,0:T(8,128)(2,1)S(1)} %fusion.70.clone.5), kind=kOutput, calls=%fused_computation.88 | convolution fusion | flops 304349184 | bytes 2167296 | tf_op jit(solution)/shard_map/dot_general | solution.py:30
  544.2 34.0 %fusion.69.clone.5 = bf16[64,512]{1,0:T(8,128)(2,1)S(1)} fusion(bf16[64,4096]{1,0:T(8,128)(2,1)S(1)} %bitcast.52, f32[512]{0:T(512)S(1)} %copy-done.4, s32[512]{0:T(512)S(1)} %copy-done.5, pred[512]{0:T(512)(128)(4,1)S(1)} %copy-done.7, f32[512]{0:T(512)S(1)} %copy-done.3), kind=kOutput, calls=%fused_computation.112.clone.clone.clone.2 | convolution fusion | flops 304152576 | bytes 596480 | tf_op jit(solution)/shard_map/dot_general | solution.py:27
  578.2 34.7 %fusion.51 = bf16[64,4096]{1,0:T(8,128)(2,1)S(1)} fusion(f32[64,4096]{1,0:T(8,128)S(1)} %convolution_add_fusion.1, f32[512]{0:T(512)S(1)} %copy-done.4, s32[512]{0:T(512)S(1)} %copy-done.5, pred[512]{0:T(512)(128)(4,1)S(1)} %copy-done.7, bf16[64,4096]{1,0:T(8,128)(2,1)S(1)} %bitcast.53, bf16[64,512]{1,0:T(8,128)(2,1)S(1)} %fusion.69.clone.5), kind=kOutput, calls=%fused_computation.94 | convolution fusion | flops 305135616 | bytes 2167296 | tf_op jit(solution)/shard_map/dot_general | solution.py:30
  612.9 4.7 copy.13
  617.6 17.1 %gather_fusion = bf16[128,16,128]{1,0,2:T(8,128)(2,1)} fusion(bf16[4,16,4096]{1,0,2:T(4,128)(2,1)} %copy.13, s32[128]{0:T(128)S(1)} %copy-done), kind=kCustom, calls=%fused_computation | custom fusion | bytes 1050112 | tf_op jit(solution)/shard_map/vmap()/gather | solution.py:45
  634.7 6.0 fusion.1
  640.8 40.7 %psum.7 = f32[16,128]{0,1:T(8,128)S(1)} all-reduce(f32[16,128]{0,1:T(8,128)S(1)} %get-tuple-element.5), channel_id=1, replica_groups=mesh['pix'=8,'chan'=4] {'pix','chan'}, use_global_device_ids=true, to_apply=%region_1.2 | all-reduce | flops 2048 | bytes 16384 | tf_op jit(solution)/shard_map/psum | solution.py:74
  681.5 0.7 copy.14
  (46 shorter events, 3.0 us)
Async XLA Ops:
  0.6 64.0 %copy-start.2 = (s32[4096]{0:T(1024)S(1)}, s32[4096]{0:T(1024)}, u32[]{:S(2)}) copy-start(s32[4096]{0:T(1024)} %param.8) | copy-start | bytes 49156
  3.2 62.0 %all-to-all-start = ((bf16[4,64,1024]{2,1,0:T(8,128)(2,1)}), bf16[4,64,1024]{2,1,0:T(8,128)(2,1)S(1)}, u32[]{:S(2)}, u32[]{:S(2)}) async-start(bf16[4,64,1024]{2,1,0:T(8,128)(2,1)} %bitcast), calls=%async_computation | async-start | bytes 1048576 | tf_op jit(solution)/shard_map/all_to_all | solution.py:58
  510.0 34.1 %copy-start.3 = (f32[512]{0:T(512)S(1)}, f32[512]{0:T(512)}, u32[]{:S(2)}) copy-start(f32[512]{0:T(512)} %get-tuple-element.8) | copy-start | bytes 6148
  510.0 34.1 %copy-start.4 = (f32[512]{0:T(512)S(1)}, f32[512]{0:T(512)}, u32[]{:S(2)}) copy-start(f32[512]{0:T(512)} %fusion.122) | copy-start | bytes 6148
  510.0 34.1 %copy-start.5 = (s32[512]{0:T(512)S(1)}, s32[512]{0:T(512)}, u32[]{:S(2)}) copy-start(s32[512]{0:T(512)} %fusion.87) | copy-start | bytes 6148
  510.0 34.1 %copy-start.7 = (pred[512]{0:T(512)(128)(4,1)S(1)}, pred[512]{0:T(512)(128)(4,1)}, u32[]{:S(2)}) copy-start(pred[512]{0:T(512)(128)(4,1)} %fusion.88) | copy-start | bytes 1540
  612.9 21.8 %copy-start.1 = (bf16[64,4096]{1,0:T(8,128)(2,1)}, bf16[64,4096]{1,0:T(8,128)(2,1)S(1)}, u32[]{:S(2)}) copy-start(bf16[64,4096]{1,0:T(8,128)(2,1)S(1)} %fusion.51) | copy-start | bytes 1572868
  612.9 4.7 copy-start
  612.9 21.8 %copy-start.6 = (pred[128]{0:T(512)(128)(4,1)S(1)}, pred[128]{0:T(512)(128)(4,1)}, u32[]{:S(2)}) copy-start(pred[128]{0:T(512)(128)(4,1)} %compare_and_fusion) | copy-start | bytes 388
where the time goes:
time: 685 us; the launch traced here: 682 us
  matrix products  547 us (80%)
  blocking collectives  87.8 us (13%)
  local copies, waits for them, and re-layouts  27.2 us (4%)
  other arithmetic  12.1 us (2%)
    dot_general x8, matrix products, filter_lines(): coeffs = jnp.dot(lines, table, preferred_element_type=jnp.float32)  274 us
    dot_general x8, matrix products, filter_lines(): lax.dot_general(kept, table, (((1,), (1,)), ((), ())), preferred_element_...  273 us
    psum x1, blocking collectives, body(): numerator = lax.psum(numerator, ('pix', 'chan'))  40.7 us
    all_gather x1, blocking collectives, body(): weights = lax.all_gather(galaxy_weight, 'pix', axis=0, tiled=True)  39.1 us
    gather x1, local copies, waits for them, and re-layouts, take(): lax.dynamic_slice(cube, (block, zero, offset.astype(jnp.int32)), (1, patc...  17.1 us
  transfers between devices with their start and end apart: 1, of which 0 were waited for; matrix products, arithmetic and copies ran while one was open for 1% of the time, Pallas kernels for 0%

commit v1 on v0

v1 whole, which is shorter than its diff:
```python
import functools
import math

import jax
import jax.numpy as jnp
import numpy as np
from jax import lax
from jax.experimental import pallas as pl
from jax.experimental.pallas import tpu as pltpu
from jax.sharding import PartitionSpec as P

MESH = pl.DeviceIdType.MESH
LANES = 128
SLABS = 32
TOTAL = LANES * SLABS
HALF = SLABS // 2
CHUNK = 16


def mode_table():
    col = np.arange(LANES)
    quarter, row = col // 32, col % 32
    is_sin, k2 = row // 16, 4 * (row % 16) + quarter
    lane = np.arange(LANES)[:, None]

    def half_block(k1):
        k = 32 * k2 + k1
        scale = np.full(LANES, math.sqrt(2.0 / TOTAL))
        phase = 2.0 * np.pi * ((lane * k[None, :]) % TOTAL) / TOTAL
        cos, sin = np.cos(phase), np.sin(phase)
        if k1 == 0:
            scale[k == 0] = math.sqrt(1.0 / TOTAL)
            edge = (is_sin == 1) & (k == 0)
            sin[:, edge] = np.where(lane % 2 == 0, 1.0, -1.0)
        return cos * scale, sin * scale

    def pick(a, b):
        return np.where(is_sin[None, :] == 1, b, a)

    blocks = np.zeros((HALF, 2 * LANES, 2 * LANES))
    for at, k1 in ((0, 0), (1, HALF)):
        cos, sin = half_block(k1)
        rows = slice(at * LANES, (at + 1) * LANES)
        blocks[0, rows, rows] = pick(cos, sin)
    for k1 in range(1, HALF):
        cos, sin = half_block(k1)
        blocks[k1, :LANES, :LANES] = pick(cos, sin)
        blocks[k1, LANES:, :LANES] = pick(sin, -cos)
        cos, sin = half_block(SLABS - k1)
        blocks[k1, :LANES, LANES:] = pick(cos, sin)
        blocks[k1, LANES:, LANES:] = pick(-sin, cos)
    return blocks.astype(jnp.bfloat16)


def times(value, c, s):
    re, im = value
    eps = 1e-12
    if abs(s) < eps and abs(c - 1) < eps:
        return value
    if abs(c) < eps and abs(s - 1) < eps:
        return (-im, re)
    if abs(c) < eps and abs(s + 1) < eps:
        return (im, -re)
    if abs(abs(c) - abs(s)) < eps:
        a = abs(c)
        sc, ss = math.copysign(1, c), math.copysign(1, s)
        t = re * (a * sc)
        u = im * (a * sc)
        return (t - u, u + t) if sc == ss else (t + u, u - t)
    return (re * c - im * s, re * s + im * c)


def real_forward(x):
    n = len(x)
    if n == 2:
        return [(x[0] + x[1], None), (x[0] - x[1], None)]
    even, odd = real_forward(x[0::2]), real_forward(x[1::2])
    half = n // 2
    out = [None] * (half + 1)
    for k in range(half // 2 + 1):
        e, o = even[k], odd[k]
        if k == 0:
            out[0] = (e[0] + o[0], None)
            out[half] = (e[0] - o[0], None)
        elif 2 * k == half:
            out[k] = (e[0], -o[0])
        else:
            angle = -2.0 * math.pi * k / n
            tr, ti = times(o, math.cos(angle), math.sin(angle))
            out[k] = (e[0] + tr, e[1] + ti)
            out[half - k] = (e[0] - tr, ti - e[1])
    return out


def real_inverse(z):
    half = len(z) - 1
    n = 2 * half
    if n == 2:
        return [z[0][0] + z[1][0], z[0][0] - z[1][0]]
    even, odd = [None] * (half // 2 + 1), [None] * (half // 2 + 1)
    for k in range(half // 2 + 1):
        a, b = z[k], z[half - k]
        if k == 0:
            even[0] = (a[0] + b[0], None)
            odd[0] = (a[0] - b[0], None)
        elif 2 * k == half:
            even[k] = (a[0] + a[0], None)
            odd[k] = (-(a[1] + a[1]), None)
        else:
            angle = 2.0 * math.pi * k / n
            even[k] = (a[0] + b[0], a[1] - b[1])
            odd[k] = times((a[0] - b[0], a[1] + b[1]), math.cos(angle), math.sin(angle))
    out = [None] * n
    out[0::2] = real_inverse(even)
    out[1::2] = real_inverse(odd)
    return out


def kernel(
    pix, chan, sky_ref, flags_ref, modes_ref, block_ref, offset_ref, weight_ref, table_ref,
    out_ref, stack_ref,
    lines, flags, weights, meta, meta_own, meta_smem, table, spec, back, cube, staged, part, sums, part2, sums2,
    flag_f, local_sem, line_send, line_recv, flag_send, flag_recv, w_send, w_recv, m_send, m_recv, s_send, s_recv,
    t_send, t_recv,
):
    me_p, me_c = lax.axis_index("pix"), lax.axis_index("chan")
    rows = lines.shape[1]
    per = SLABS // chan
    count = weights.shape[1]
    patch = weights.shape[2]

    own = [
        pltpu.make_async_copy(table_ref, table, local_sem.at[0]),
        pltpu.make_async_copy(sky_ref.at[pl.ds(pl.multiple_of(me_c * rows, rows), rows)], lines.at[me_c], local_sem.at[1]),
        pltpu.make_async_copy(flags_ref, flags.at[me_c], local_sem.at[2]),
        pltpu.make_async_copy(weight_ref, weights.at[me_p], local_sem.at[3]),
    ]
    for copy in own:
        copy.start()
    meta_own[0:1, 0:count] = block_ref[...]
    meta_own[1:2, 0:count] = offset_ref[...]

    barrier = pltpu.get_barrier_semaphore()
    chan_peers = [lax.rem(me_c + d, chan) for d in range(1, chan)]
    pix_peers = [lax.rem(me_p + d, pix) for d in range(1, pix)]
    for c in chan_peers:
        pl.semaphore_signal(barrier, inc=1, device_id=(me_p, c), device_id_type=MESH)
    for p in pix_peers:
        pl.semaphore_signal(barrier, inc=1, device_id=(p, me_c), device_id_type=MESH)
    pl.semaphore_wait(barrier, chan + pix - 2)

    def remote(src, dst, send, recv, device):
        return pltpu.make_async_remote_copy(
            src_ref=src, dst_ref=dst, send_sem=send, recv_sem=recv, device_id=device, device_id_type=MESH
        )

    line_copies, flag_copies, w_copies, m_copies = [], [], [], []
    for i, c in enumerate(chan_peers):
        line_copies.append(
            remote(
                sky_ref.at[pl.ds(pl.multiple_of(c * rows, rows), rows)], lines.at[me_c],
                line_send.at[i], line_recv.at[i], (me_p, c),
            )
        )
        line_copies[-1].start()
    for i, p in enumerate(pix_peers):
        m_copies.append(remote(meta_own, meta.at[me_p], m_send.at[i], m_recv.at[i], (p, me_c)))
        m_copies[-1].start()
        w_copies.append(remote(weight_ref, weights.at[me_p], w_send.at[i], w_recv.at[i], (p, me_c)))
        w_copies[-1].start()
    for i, c in enumerate(chan_peers):
        flag_copies.append(remote(flags_ref, flags.at[me_c], flag_send.at[i], flag_recv.at[i], (me_p, c)))
        flag_copies[-1].start()

    modes = modes_ref[...].astype(jnp.float32)
    eye = (
        lax.broadcasted_iota(jnp.int32, (LANES, LANES), 0) == lax.broadcasted_iota(jnp.int32, (LANES, LANES), 1)
    ).astype(jnp.float32)
    turned = lax.dot_general(eye, modes, (((1,), (1,)), ((), ())), preferred_element_type=jnp.float32)
    mask = jnp.zeros((32, LANES), jnp.float32)
    for q in range(4):
        place = (
            lax.broadcasted_iota(jnp.int32, (32, LANES), 1) == lax.broadcasted_iota(jnp.int32, (32, LANES), 0) + 32 * q
        ).astype(jnp.float32)
        mask = mask + jnp.dot(turned[32 * q : 32 * q + 32], place, preferred_element_type=jnp.float32)

    meta[me_p] = meta_own[...]
    for copy in m_copies:
        copy.wait()
    to_smem = pltpu.make_async_copy(meta, meta_smem, local_sem.at[4])
    to_smem.start()
    for copy in own:
        copy.wait()
    for copy in w_copies:
        copy.wait()
    to_smem.wait()

    def add_power(i, acc):
        w = weights[i].astype(jnp.float32)
        return acc + jnp.sum(w * w, axis=0)

    power = lax.fori_loop(0, pix, add_power, jnp.zeros((patch, LANES), jnp.float32))

    for copy in flag_copies:
        copy.wait()
    for c in range(chan):
        flag_f[c * per : (c + 1) * per, :] = flags[c].astype(jnp.float32)
    for copy in line_copies:
        copy.wait()

    def slab(n1, at):
        c, s = n1 // per, n1 % per
        value = lines[c, pl.ds(at, CHUNK), s * LANES : (s + 1) * LANES].astype(jnp.float32)
        return value * flag_f[n1 : n1 + 1, :]

    def forward(i, carry):
        at = pl.multiple_of(i * CHUNK, CHUNK)
        y = real_forward([slab(n1, at) for n1 in range(SLABS)])
        spec[0, pl.ds(at, CHUNK), :LANES] = y[0][0].astype(jnp.bfloat16)
        spec[0, pl.ds(at, CHUNK), LANES:] = y[HALF][0].astype(jnp.bfloat16)
        for k in range(1, HALF):
            spec[k, pl.ds(at, CHUNK), :LANES] = y[k][0].astype(jnp.bfloat16)
            spec[k, pl.ds(at, CHUNK), LANES:] = y[k][1].astype(jnp.bfloat16)
        return carry

    lax.fori_loop(0, rows // CHUNK, forward, 0)

    for k in range(HALF):
        other = HALF if k == 0 else SLABS - k
        gain = 1.0 if k == 0 else 0.5
        chosen = jnp.concatenate([mask[k : k + 1], mask[other : other + 1]], axis=1) * gain
        coeffs = jnp.dot(spec[k], table[k], preferred_element_type=jnp.float32)
        kept = (coeffs * chosen).astype(jnp.bfloat16)
        back[k] = lax.dot_general(kept, table[k], (((1,), (1,)), ((), ())), preferred_element_type=jnp.float32)

    def inverse(i, carry):
        at = pl.multiple_of(i * CHUNK, CHUNK)
        here = pl.ds(at, CHUNK)
        z = [(back[0, here, :LANES], None)]
        z += [(back[k, here, :LANES], back[k, here, LANES:]) for k in range(1, HALF)]
        z += [(back[0, here, LANES:], None)]
        ripple = real_inverse(z)
        for n1 in range(SLABS):
            value = (slab(n1, at) - ripple[n1]).astype(jnp.bfloat16)
            staged[here, n1 * LANES : (n1 + 1) * LANES] = value
            cube[i * SLABS + n1] = value.astype(jnp.float32)
        return carry

    lax.fori_loop(0, rows // CHUNK, inverse, 0)
    result = pltpu.make_async_copy(staged, out_ref, local_sem.at[5])
    result.start()

    here_blocks = rows // patch
    first = (me_p * chan + me_c) * here_blocks
    lane = lax.broadcasted_iota(jnp.int32, (patch, LANES), 1)

    def add_panels(p, acc):
        for g in range(count):
            local = meta_smem[p, 0, g] - first
            offset = meta_smem[p, 1, g]
            safe = jnp.clip(local, 0, here_blocks - 1)
            owned = local == safe
            base = offset // LANES
            shift = offset - base * LANES
            low = cube[safe * SLABS + base]
            high = cube[safe * SLABS + jnp.minimum(base + 1, SLABS - 1)]
            joined = jnp.where(lane >= shift, low, high)
            panel = pltpu.roll(joined, lax.rem(LANES - shift, LANES), 1)
            w = weights[p, g].astype(jnp.float32)
            acc = acc + jnp.where(owned, w * panel, 0.0)
        return acc

    total = lax.fori_loop(0, pix, add_panels, jnp.zeros((patch, LANES), jnp.float32))

    part[...] = total
    sends = [
        remote(part, sums.at[me_p], s_send.at[i], s_recv.at[i], (p, me_c)) for i, p in enumerate(pix_peers)
    ]
    for copy in sends:
        copy.start()
    sums[me_p] = total
    for copy in sends:
        copy.wait()
    total = jnp.sum(sums[...], axis=0)
    part2[...] = total
    sends = [
        remote(part2, sums2.at[me_c], t_send.at[i], t_recv.at[i], (me_p, c)) for i, c in enumerate(chan_peers)
    ]
    for copy in sends:
        copy.start()
    sums2[me_c] = total
    for copy in sends:
        copy.wait()
    stack_ref[...] = jnp.sum(sums2[...], axis=0) / jnp.sqrt(power)
    result.wait()


def solution(mesh):
    pix, chan = mesh.shape["pix"], mesh.shape["chan"]

    def body(sky_map, channel_flags, ripple_modes, galaxy_block, galaxy_offset, galaxy_weight):
        rows = sky_map.shape[0] // chan
        width = sky_map.shape[1]
        count, patch, _ = galaxy_weight.shape
        per = width // LANES
        any_spec = pl.BlockSpec(memory_space=pl.ANY)
        vmem_spec = pl.BlockSpec(memory_space=pltpu.VMEM)
        dma = pltpu.SemaphoreType.DMA
        table = jnp.asarray(mode_table())
        return pl.pallas_call(
            functools.partial(kernel, pix, chan),
            out_shape=(
                jax.ShapeDtypeStruct((rows, TOTAL), jnp.bfloat16),
                jax.ShapeDtypeStruct((patch, LANES), jnp.float32),
            ),
            in_specs=[any_spec, any_spec, vmem_spec, vmem_spec, vmem_spec, any_spec, any_spec],
            out_specs=(any_spec, vmem_spec),
            scratch_shapes=[
                pltpu.VMEM((chan, rows, width), jnp.bfloat16),
                pltpu.VMEM((chan, per, LANES), jnp.int32),
                pltpu.VMEM((pix, count, patch, LANES), jnp.bfloat16),
                pltpu.VMEM((pix, 8, LANES), jnp.int32),
                pltpu.VMEM((8, LANES), jnp.int32),
                pltpu.SMEM((pix, 8, LANES), jnp.int32),
                pltpu.VMEM((HALF, 2 * LANES, 2 * LANES), jnp.bfloat16),
                pltpu.VMEM((HALF, rows, 2 * LANES), jnp.bfloat16),
                pltpu.VMEM((HALF, rows, 2 * LANES), jnp.float32),
                pltpu.VMEM((rows // patch * SLABS, patch, LANES), jnp.float32),
                pltpu.VMEM((rows, TOTAL), jnp.bfloat16),
                pltpu.VMEM((patch, LANES), jnp.float32),
                pltpu.VMEM((pix, patch, LANES), jnp.float32),
                pltpu.VMEM((patch, LANES), jnp.float32),
                pltpu.VMEM((chan, patch, LANES), jnp.float32),
                pltpu.VMEM((SLABS, LANES), jnp.float32),
                dma((6,)),
                dma((chan - 1,)), dma((chan - 1,)), dma((chan - 1,)), dma((chan - 1,)),
                dma((pix - 1,)), dma((pix - 1,)), dma((pix - 1,)), dma((pix - 1,)),
                dma((pix - 1,)), dma((pix - 1,)),
                dma((chan - 1,)), dma((chan - 1,)),
            ],
            compiler_params=pltpu.CompilerParams(collective_id=0, has_side_effects=True),
        )(
            sky_map, channel_flags.reshape(per, LANES), ripple_modes.reshape(32, LANES),
            galaxy_block.reshape(1, count), galaxy_offset.reshape(1, count), galaxy_weight, table,
        )

    in_specs = (P("pix", "chan"), P("chan"), P(), P("pix"), P("pix"), P("pix", None, None))
    out_specs = (P(("pix", "chan"), None), P())
    return jax.shard_map(body, mesh=mesh, in_specs=in_specs, out_specs=out_specs, check_vma=False)
```

time: 685 us -> 36.3 us (0.05)
  matrix products: 547 us -> 0 us
  blocking collectives: 87.8 us -> 0 us
  Pallas kernels: 0 us -> 32.3 us
  local copies, waits for them, and re-layouts: 27.2 us -> 3.16 us
  other arithmetic: 12.1 us -> 0 us
    dot_general x16 -> x0, matrix products: 547 us -> none  [the longest x8 274 us: filter_lines(): coeffs = jnp.dot(lines, table, preferred_element_type=jnp.float32)]
    psum x1 -> x0, blocking collectives: 40.7 us -> none  [body(): numerator = lax.psum(numerator, ('pix', 'chan'))]
    all_gather x1 -> x0, blocking collectives: 39.1 us -> none  [body(): weights = lax.all_gather(galaxy_weight, 'pix', axis=0, tiled=True)]
    pallas_call x0 -> x1, Pallas kernels: none -> 32.3 us  [body(): pl.pallas_call(functools.partial(kernel, pix, chan), out_shape=(jax.Shape...]
    gather x1 -> x0, local copies, waits for them, and re-layouts: 17.1 us -> none  [take(): lax.dynamic_slice(cube, (block, zero, offset.astype(jnp.int32)), (1, patc...]
    unnamed x1 -> x0, blocking collectives: 8.01 us -> none
  transfers between devices with their start and end apart: 1 -> 0, of which waited for: 0 -> 0; matrix products, arithmetic and copies ran while one was open for 1% -> 0% of each run, Pallas kernels for 0% -> 0%
where the time goes in v1:
time: 36.3 us; the launch traced here: 36.1 us
  Pallas kernels  32.3 us (89%)
  local copies, waits for them, and re-layouts  3.16 us (9%)
  between operations  0.64 us (2%)
    pallas_call x1, Pallas kernels, body(): pl.pallas_call(functools.partial(kernel, pix, chan), out_shape=(jax.Shape...  32.3 us
    unnamed x2, local copies, waits for them, and re-layouts  3.16 us

profile of v1, /device:TPU:0, one launch (start us, length us, event | category | flops | bytes accessed | tf_op | source)
XLA Modules:
  0.0 36.1 jit_solution(4241224456384032330)
XLA Ops:
  0.6 32.3 %shard_map.86 = (bf16[64,4096]{1,0:T(8,128)(2,1)}, f32[16,128]{1,0:T(8,128)}) custom-call(bf16[256,1024]{1,0:T(8,128)(2,1)} %sky_ref.1, s32[8,128]{1,0:T(8,128)} %bitcast.5, s32[32,128]{1,0:T(8,128)} %bitcast.4, s32[1,16]{1,0:T(1,128)} %bitcast.6, s32[1,16]{1,0:T(1,128)} %bitcast.7, bf16[16,16,128]{2,1,0:T(8,128)(2,1)} %weight_ref.1, ...), custom_call_target="tpu_custom_call" | custom-call | tf_op jit(solution)/shard_map/pallas_call | solution.py:310
  32.9 1.9 %copy.11 = bf16[64,4096]{1,0:T(8,128)(2,1)} copy(bf16[64,4096]{1,0:T(8,128)(2,1)} %get-tuple-element.4) | data formatting | bytes 1048576
  34.8 1.3 %copy.12 = f32[16,128]{1,0:T(8,128)} copy(f32[16,128]{1,0:T(8,128)} %get-tuple-element.5) | data formatting | bytes 16384

commit v2 on v1

v2 whole, which is shorter than its diff:
```python
import functools
import math

import jax
import jax.numpy as jnp
import numpy as np
from jax import lax
from jax.experimental import pallas as pl
from jax.experimental.pallas import tpu as pltpu
from jax.sharding import PartitionSpec as P

MESH = pl.DeviceIdType.MESH
LANES = 128
SLABS = 32
TOTAL = LANES * SLABS
HALF = SLABS // 2
CHUNK = 16
STEP = 16


def mode_table():
    col = np.arange(LANES)
    quarter, row = col // 32, col % 32
    is_sin, k2 = row // 16, 4 * (row % 16) + quarter
    lane = np.arange(LANES)[:, None]

    def half_block(k1):
        k = 32 * k2 + k1
        scale = np.full(LANES, math.sqrt(2.0 / TOTAL))
        phase = 2.0 * np.pi * ((lane * k[None, :]) % TOTAL) / TOTAL
        cos, sin = np.cos(phase), np.sin(phase)
        if k1 == 0:
            scale[k == 0] = math.sqrt(1.0 / TOTAL)
            edge = (is_sin == 1) & (k == 0)
            sin[:, edge] = np.where(lane % 2 == 0, 1.0, -1.0)
        return cos * scale, sin * scale

    def pick(a, b):
        return np.where(is_sin[None, :] == 1, b, a)

    blocks = np.zeros((HALF, 2 * LANES, 2 * LANES))
    for at, k1 in ((0, 0), (1, HALF)):
        cos, sin = half_block(k1)
        rows = slice(at * LANES, (at + 1) * LANES)
        blocks[0, rows, rows] = pick(cos, sin)
    for k1 in range(1, HALF):
        cos, sin = half_block(k1)
        blocks[k1, :LANES, :LANES] = pick(cos, sin)
        blocks[k1, LANES:, :LANES] = pick(sin, -cos)
        cos, sin = half_block(SLABS - k1)
        blocks[k1, :LANES, LANES:] = pick(cos, sin)
        blocks[k1, LANES:, LANES:] = pick(-sin, cos)
    return blocks.astype(jnp.bfloat16)


def times(value, c, s):
    re, im = value
    eps = 1e-12
    if abs(s) < eps and abs(c - 1) < eps:
        return value
    if abs(c) < eps and abs(s - 1) < eps:
        return (-im, re)
    if abs(c) < eps and abs(s + 1) < eps:
        return (im, -re)
    if abs(abs(c) - abs(s)) < eps:
        a = abs(c)
        sc, ss = math.copysign(1, c), math.copysign(1, s)
        t = re * (a * sc)
        u = im * (a * sc)
        return (t - u, u + t) if sc == ss else (t + u, u - t)
    return (re * c - im * s, re * s + im * c)


def real_forward(x):
    n = len(x)
    if n == 2:
        return [(x[0] + x[1], None), (x[0] - x[1], None)]
    even, odd = real_forward(x[0::2]), real_forward(x[1::2])
    half = n // 2
    out = [None] * (half + 1)
    for k in range(half // 2 + 1):
        e, o = even[k], odd[k]
        if k == 0:
            out[0] = (e[0] + o[0], None)
            out[half] = (e[0] - o[0], None)
        elif 2 * k == half:
            out[k] = (e[0], -o[0])
        else:
            angle = -2.0 * math.pi * k / n
            tr, ti = times(o, math.cos(angle), math.sin(angle))
            out[k] = (e[0] + tr, e[1] + ti)
            out[half - k] = (e[0] - tr, ti - e[1])
    return out


def real_inverse(z):
    half = len(z) - 1
    n = 2 * half
    if n == 2:
        return [z[0][0] + z[1][0], z[0][0] - z[1][0]]
    even, odd = [None] * (half // 2 + 1), [None] * (half // 2 + 1)
    for k in range(half // 2 + 1):
        a, b = z[k], z[half - k]
        if k == 0:
            even[0] = (a[0] + b[0], None)
            odd[0] = (a[0] - b[0], None)
        elif 2 * k == half:
            even[k] = (a[0] + a[0], None)
            odd[k] = (-(a[1] + a[1]), None)
        else:
            angle = 2.0 * math.pi * k / n
            even[k] = (a[0] + b[0], a[1] - b[1])
            odd[k] = times((a[0] - b[0], a[1] + b[1]), math.cos(angle), math.sin(angle))
    out = [None] * n
    out[0::2] = real_inverse(even)
    out[1::2] = real_inverse(odd)
    return out


def kernel(
    pix, chan, sky_ref, flags_ref, modes_ref, block_ref, offset_ref, weight_ref, table_ref,
    out_ref, stack_ref,
    lines, flags, modes_v, block_v, offset_v, weights, chosen_w, meta, meta_own, meta_smem, table, spec, back, cube, staged,
    part, sums, part2, sums2, flag_f, mask_ref, local_sem, out_sem, line_send, line_recv, flag_send, flag_recv,
    w_send, w_recv, m_send, m_recv, s_send, s_recv, t_send, t_recv,
):
    me_p, me_c = lax.axis_index("pix"), lax.axis_index("chan")
    rows = lines.shape[1]
    per = SLABS // chan
    count = weights.shape[1]
    patch = weights.shape[2]
    steps = rows // STEP

    barrier = pltpu.get_barrier_semaphore()
    chan_peers = [lax.rem(me_c + d, chan) for d in range(1, chan)]
    pix_peers = [lax.rem(me_p + d, pix) for d in range(1, pix)]
    for c in chan_peers:
        pl.semaphore_signal(barrier, inc=1, device_id=(me_p, c), device_id_type=MESH)
    for p in pix_peers:
        pl.semaphore_signal(barrier, inc=1, device_id=(p, me_c), device_id_type=MESH)

    own = [
        pltpu.make_async_copy(table_ref, table, local_sem.at[0]),
        pltpu.make_async_copy(sky_ref.at[pl.ds(pl.multiple_of(me_c * rows, rows), rows)], lines.at[me_c], local_sem.at[1]),
        pltpu.make_async_copy(flags_ref, flags.at[me_c], local_sem.at[2]),
        pltpu.make_async_copy(weight_ref, weights.at[me_p], local_sem.at[3]),
        pltpu.make_async_copy(modes_ref, modes_v, local_sem.at[5]),
    ]
    places = [
        pltpu.make_async_copy(block_ref, block_v, local_sem.at[6]),
        pltpu.make_async_copy(offset_ref, offset_v, local_sem.at[7]),
    ]
    for copy in places + own:
        copy.start()
    for copy in places:
        copy.wait()
    meta_own[0:1, 0:count] = block_v[...]
    meta_own[1:2, 0:count] = offset_v[...]
    pl.semaphore_wait(barrier, chan + pix - 2)

    def remote(src, dst, send, recv, device):
        return pltpu.make_async_remote_copy(
            src_ref=src, dst_ref=dst, send_sem=send, recv_sem=recv, device_id=device, device_id_type=MESH
        )

    def line_copy(i, c, step):
        there = pl.ds(pl.multiple_of(c * rows + step * STEP, STEP), STEP)
        here = pl.ds(pl.multiple_of(step * STEP, STEP), STEP)
        return remote(
            sky_ref.at[there], lines.at[me_c, here], line_send.at[step, i], line_recv.at[step, i], (me_p, c)
        )

    flag_copies, w_copies, m_copies = [], [], []
    for step in range(steps):
        for i, c in enumerate(chan_peers):
            if step == 0:
                flag_copies.append(remote(flags_ref, flags.at[me_c], flag_send.at[i], flag_recv.at[i], (me_p, c)))
                flag_copies[-1].start()
            line_copy(i, c, step).start()
    for i, p in enumerate(pix_peers):
        m_copies.append(remote(meta_own, meta.at[me_p], m_send.at[i], m_recv.at[i], (p, me_c)))
        m_copies[-1].start()
        w_copies.append(remote(weight_ref, weights.at[me_p], w_send.at[i], w_recv.at[i], (p, me_c)))
        w_copies[-1].start()

    for copy in own:
        copy.wait()
    modes = modes_v[...].astype(jnp.float32)
    eye = (
        lax.broadcasted_iota(jnp.int32, (LANES, LANES), 0) == lax.broadcasted_iota(jnp.int32, (LANES, LANES), 1)
    ).astype(jnp.float32)
    turned = lax.dot_general(eye, modes, (((1,), (1,)), ((), ())), preferred_element_type=jnp.float32)
    mask = jnp.zeros((32, LANES), jnp.float32)
    for q in range(4):
        place = (
            lax.broadcasted_iota(jnp.int32, (32, LANES), 1) == lax.broadcasted_iota(jnp.int32, (32, LANES), 0) + 32 * q
        ).astype(jnp.float32)
        mask = mask + jnp.dot(turned[32 * q : 32 * q + 32], place, preferred_element_type=jnp.float32)
    mask_ref[...] = mask

    for copy in flag_copies:
        copy.wait()
    for c in range(chan):
        flag_f[c * per : (c + 1) * per, :] = flags[c].astype(jnp.float32)

    meta[me_p] = meta_own[...]
    for copy in m_copies:
        copy.wait()
    to_smem = pltpu.make_async_copy(meta, meta_smem, local_sem.at[4])
    to_smem.start()
    for copy in w_copies:
        copy.wait()
    to_smem.wait()

    here_blocks = rows // patch
    first = (me_p * chan + me_c) * here_blocks

    def choose(p, acc):
        for g in range(count):
            local = meta_smem[p, 0, g] - first
            safe = jnp.clip(local, 0, here_blocks - 1)
            offset = meta_smem[p, 1, g]
            base = lax.div(offset, LANES)
            shift = offset - base * LANES
            meta_smem[p, 2, g] = safe * SLABS + base
            meta_smem[p, 3, g] = safe * SLABS + jnp.minimum(base + 1, SLABS - 1)
            meta_smem[p, 4, g] = shift
            w = weights[p, g].astype(jnp.float32)
            acc = acc + w * w
            chosen_w[p, g] = jnp.where(local == safe, w, 0.0)
        return acc

    power = lax.fori_loop(0, pix, choose, jnp.zeros((patch, LANES), jnp.float32))

    def slab(n1, at):
        c, s = n1 // per, n1 % per
        value = lines[c, pl.ds(at, CHUNK), s * LANES : (s + 1) * LANES].astype(jnp.float32)
        return value * flag_f[n1 : n1 + 1, :]

    def filter_rows(step, carry):
        for i, c in enumerate(chan_peers):
            line_copy(i, c, step).wait_recv()
        for j in range(STEP // CHUNK):
            at = pl.multiple_of(step * STEP + j * CHUNK, CHUNK)
            r = slice(j * CHUNK, (j + 1) * CHUNK)
            y = real_forward([slab(n1, at) for n1 in range(SLABS)])
            spec[0, r, :LANES] = y[0][0].astype(jnp.bfloat16)
            spec[0, r, LANES:] = y[HALF][0].astype(jnp.bfloat16)
            for k in range(1, HALF):
                spec[k, r, :LANES] = y[k][0].astype(jnp.bfloat16)
                spec[k, r, LANES:] = y[k][1].astype(jnp.bfloat16)
        for k in range(HALF):
            other = HALF if k == 0 else SLABS - k
            gain = 1.0 if k == 0 else 0.5
            chosen = jnp.concatenate([mask_ref[k : k + 1], mask_ref[other : other + 1]], axis=1) * gain
            coeffs = jnp.dot(spec[k], table[k], preferred_element_type=jnp.float32)
            kept = (coeffs * chosen).astype(jnp.bfloat16)
            back[k] = lax.dot_general(kept, table[k], (((1,), (1,)), ((), ())), preferred_element_type=jnp.float32)
        for j in range(STEP // CHUNK):
            at = pl.multiple_of(step * STEP + j * CHUNK, CHUNK)
            r = slice(j * CHUNK, (j + 1) * CHUNK)
            z = [(back[0, r, :LANES], None)]
            z += [(back[k, r, :LANES], back[k, r, LANES:]) for k in range(1, HALF)]
            z += [(back[0, r, LANES:], None)]
            ripple = real_inverse(z)
            for n1 in range(SLABS):
                value = (slab(n1, at) - ripple[n1]).astype(jnp.bfloat16)
                staged[pl.ds(at, CHUNK), n1 * LANES : (n1 + 1) * LANES] = value
                cube[(step * (STEP // CHUNK) + j) * SLABS + n1] = value.astype(jnp.float32)
        here = pl.ds(pl.multiple_of(step * STEP, STEP), STEP)
        pltpu.make_async_copy(staged.at[here], out_ref.at[here], out_sem.at[step]).start()
        return carry

    lax.fori_loop(0, steps, filter_rows, 0)

    lane = lax.broadcasted_iota(jnp.int32, (patch, LANES), 1)

    def add_panels(p, acc):
        for g in range(count):
            low = cube[meta_smem[p, 2, g]]
            high = cube[meta_smem[p, 3, g]]
            shift = meta_smem[p, 4, g]
            joined = jnp.where(lane >= shift, low, high)
            panel = pltpu.roll(joined, lax.rem(LANES - shift, LANES), 1)
            acc = acc + chosen_w[p, g] * panel
        return acc

    total = lax.fori_loop(0, pix, add_panels, jnp.zeros((patch, LANES), jnp.float32))

    part[...] = total
    sends = [
        remote(part, sums.at[me_p], s_send.at[i], s_recv.at[i], (p, me_c)) for i, p in enumerate(pix_peers)
    ]
    for copy in sends:
        copy.start()
    sums[me_p] = total
    for copy in sends:
        copy.wait()
    total = jnp.sum(sums[...], axis=0)
    part2[...] = total
    sends = [
        remote(part2, sums2.at[me_c], t_send.at[i], t_recv.at[i], (me_p, c)) for i, c in enumerate(chan_peers)
    ]
    for copy in sends:
        copy.start()
    sums2[me_c] = total
    for step in range(steps):
        for i, c in enumerate(chan_peers):
            line_copy(i, c, step).wait_send()
        here = pl.ds(step * STEP, STEP)
        pltpu.make_async_copy(staged.at[here], out_ref.at[here], out_sem.at[step]).wait()
    for copy in sends:
        copy.wait()
    stack_ref[...] = jnp.sum(sums2[...], axis=0) / jnp.sqrt(power)


def hand_over(filtered_ref, stack_ref, out_ref, stack_out, sem):
    copy = pltpu.make_async_copy(filtered_ref, out_ref, sem)
    copy.start()
    stack_out[...] = stack_ref[...]
    copy.wait()


def solution(mesh):
    pix, chan = mesh.shape["pix"], mesh.shape["chan"]

    def body(sky_map, channel_flags, ripple_modes, galaxy_block, galaxy_offset, galaxy_weight):
        rows = sky_map.shape[0] // chan
        width = sky_map.shape[1]
        count, patch, _ = galaxy_weight.shape
        per = width // LANES
        any_spec = pl.BlockSpec(memory_space=pl.ANY)
        vmem_spec = pl.BlockSpec(memory_space=pltpu.VMEM)
        dma = pltpu.SemaphoreType.DMA
        table = jnp.asarray(mode_table())
        shapes = (
            jax.ShapeDtypeStruct((rows, TOTAL), jnp.bfloat16),
            jax.ShapeDtypeStruct((patch, LANES), jnp.float32),
        )
        filtered, stack = pl.pallas_call(
            functools.partial(kernel, pix, chan),
            out_shape=shapes,
            in_specs=[pl.BlockSpec(memory_space=pltpu.HBM)] * 7,
            out_specs=(any_spec, vmem_spec),
            scratch_shapes=[
                pltpu.VMEM((chan, rows, width), jnp.bfloat16),
                pltpu.VMEM((chan, per, LANES), jnp.int32),
                pltpu.VMEM((32, LANES), jnp.int32),
                pltpu.VMEM((1, count), jnp.int32),
                pltpu.VMEM((1, count), jnp.int32),
                pltpu.VMEM((pix, count, patch, LANES), jnp.bfloat16),
                pltpu.VMEM((pix, count, patch, LANES), jnp.float32),
                pltpu.VMEM((pix, 8, LANES), jnp.int32),
                pltpu.VMEM((8, LANES), jnp.int32),
                pltpu.SMEM((pix, 8, LANES), jnp.int32),
                pltpu.VMEM((HALF, 2 * LANES, 2 * LANES), jnp.bfloat16),
                pltpu.VMEM((HALF, STEP, 2 * LANES), jnp.bfloat16),
                pltpu.VMEM((HALF, STEP, 2 * LANES), jnp.float32),
                pltpu.VMEM((rows // patch * SLABS, patch, LANES), jnp.float32),
                pltpu.VMEM((rows, TOTAL), jnp.bfloat16),
                pltpu.VMEM((patch, LANES), jnp.float32),
                pltpu.VMEM((pix, patch, LANES), jnp.float32),
                pltpu.VMEM((patch, LANES), jnp.float32),
                pltpu.VMEM((chan, patch, LANES), jnp.float32),
                pltpu.VMEM((SLABS, LANES), jnp.float32),
                pltpu.VMEM((SLABS, LANES), jnp.float32),
                dma((8,)), dma((rows // STEP,)),
                dma((rows // STEP, chan - 1)), dma((rows // STEP, chan - 1)), dma((chan - 1,)), dma((chan - 1,)),
                dma((pix - 1,)), dma((pix - 1,)), dma((pix - 1,)), dma((pix - 1,)),
                dma((pix - 1,)), dma((pix - 1,)),
                dma((chan - 1,)), dma((chan - 1,)),
            ],
            compiler_params=pltpu.CompilerParams(collective_id=0, has_side_effects=True, vmem_limit_bytes=32 << 20),
        )(
            *(pltpu.with_memory_space_constraint(v, pltpu.HBM) for v in (
            sky_map, channel_flags.reshape(per, LANES), ripple_modes.reshape(32, LANES),
            galaxy_block.reshape(1, count), galaxy_offset.reshape(1, count), galaxy_weight, table,
            ))
        )
        return pl.pallas_call(
            hand_over,
            out_shape=shapes,
            in_specs=[any_spec, vmem_spec],
            out_specs=(any_spec, vmem_spec),
            scratch_shapes=[dma(())],
            compiler_params=pltpu.CompilerParams(vmem_limit_bytes=2 << 20),
        )(filtered, stack)

    in_specs = (P("pix", "chan"), P("chan"), P(), P("pix"), P("pix"), P("pix", None, None))
    out_specs = (P(("pix", "chan"), None), P())
    return jax.shard_map(body, mesh=mesh, in_specs=in_specs, out_specs=out_specs, check_vma=False)
```

time: 36.3 us -> 33.3 us (0.917)
  local copies, waits for them, and re-layouts: 3.16 us -> 0 us
    unnamed x2 -> x0, local copies, waits for them, and re-layouts: 3.16 us -> none
    pallas_call x1 -> x2, Pallas kernels: 32.3 us -> 32.5 us  [the longest x1 31.1 us: body(): pl.pallas_call(functools.partial(kernel, pix, chan), out_shape=shapes, in...]
where the time goes in v2:
time: 33.3 us; the launch traced here: 33.1 us
  Pallas kernels  32.5 us (98%)
  between operations  0.64 us (2%)
    pallas_call x1, Pallas kernels, body(): pl.pallas_call(functools.partial(kernel, pix, chan), out_shape=shapes, in...  31.1 us
    pallas_call x1, Pallas kernels, body(): pl.pallas_call(hand_over, out_shape=shapes, in_specs=[any_spec, vmem_spec...  1.4 us

profile of v2, /device:TPU:0, one launch (start us, length us, event | category | flops | bytes accessed | tf_op | source)
XLA Modules:
  0.0 33.1 jit_solution(13769173618096855670)
XLA Ops:
  0.6 31.1 %shard_map.86 = (bf16[64,4096]{1,0:T(8,128)(2,1)S(1)}, f32[16,128]{1,0:T(8,128)S(1)}) custom-call(bf16[256,1024]{1,0:T(8,128)(2,1)} %sky_ref.1, s32[8,128]{1,0:T(8,128)} %bitcast.5, s32[32,128]{1,0:T(8,128)} %bitcast.4, s32[1,16]{1,0:T(1,128)} %bitcast.6, s32[1,16]{1,0:T(1,128)} %bitcast.7, bf16[16,16,128]{2,1,0:T(8,128)(2,1)} %weight_ref.1, ...), custom_call_target="tpu_custom_call" | custom-call | tf_op jit(solution)/shard_map/pallas_call | solution.py:340
  31.7 1.4 %shard_map.87 = (bf16[64,4096]{1,0:T(8,128)(2,1)}, f32[16,128]{1,0:T(8,128)}) custom-call(bf16[64,4096]{1,0:T(8,128)(2,1)S(1)} %get-tuple-element.4.filtered_ref, f32[16,128]{1,0:T(8,128)S(1)} %get-tuple-element.5.stack_ref), custom_call_target="tpu_custom_call" | custom-call | tf_op jit(solution)/shard_map/pallas_call | solution.py:380

commit v3 on v2

--- a/solution.py
+++ b/solution.py
@@ -18,39 +18,32 @@
 STEP = 16
 
 
-def mode_table():
+def mode_tables():
     col = np.arange(LANES)
     quarter, row = col // 32, col % 32
-    is_sin, k2 = row // 16, 4 * (row % 16) + quarter
+    is_sin, k2 = (row // 16 == 1)[None, :], 4 * (row % 16) + quarter
     lane = np.arange(LANES)[:, None]
 
-    def half_block(k1):
-        k = 32 * k2 + k1
-        scale = np.full(LANES, math.sqrt(2.0 / TOTAL))
+    def waves(k):
         phase = 2.0 * np.pi * ((lane * k[None, :]) % TOTAL) / TOTAL
-        cos, sin = np.cos(phase), np.sin(phase)
-        if k1 == 0:
-            scale[k == 0] = math.sqrt(1.0 / TOTAL)
-            edge = (is_sin == 1) & (k == 0)
-            sin[:, edge] = np.where(lane % 2 == 0, 1.0, -1.0)
-        return cos * scale, sin * scale
-
-    def pick(a, b):
-        return np.where(is_sin[None, :] == 1, b, a)
-
-    blocks = np.zeros((HALF, 2 * LANES, 2 * LANES))
-    for at, k1 in ((0, 0), (1, HALF)):
-        cos, sin = half_block(k1)
-        rows = slice(at * LANES, (at + 1) * LANES)
-        blocks[0, rows, rows] = pick(cos, sin)
-    for k1 in range(1, HALF):
-        cos, sin = half_block(k1)
-        blocks[k1, :LANES, :LANES] = pick(cos, sin)
-        blocks[k1, LANES:, :LANES] = pick(sin, -cos)
-        cos, sin = half_block(SLABS - k1)
-        blocks[k1, :LANES, LANES:] = pick(cos, sin)
-        blocks[k1, LANES:, LANES:] = pick(-sin, cos)
-    return blocks.astype(jnp.bfloat16)
+        return np.cos(phase) * math.sqrt(2.0 / TOTAL), np.sin(phase) * math.sqrt(2.0 / TOTAL)
+
+    tables = np.zeros((4, 2 * LANES, 2 * LANES))
+    cos, sin = waves(32 * k2)
+    cos[:, k2 == 0] *= math.sqrt(0.5)
+    sin[:, k2 == 0] = np.where(lane % 2 == 0, 1.0, -1.0) * math.sqrt(1.0 / TOTAL)
+    tables[0, :LANES, :LANES] = np.where(is_sin, sin, cos)
+    cos, sin = waves(32 * k2 + 16)
+    tables[0, LANES:, LANES:] = np.where(is_sin, sin, cos)
+    cos, sin = waves(32 * k2)
+    tables[1, :LANES, :LANES] = np.where(is_sin, sin, cos)
+    tables[1, LANES:, :LANES] = np.where(is_sin, -cos, sin)
+    cos, sin = waves(32 * (LANES - 1 - k2))
+    tables[1, :LANES, LANES:] = np.where(is_sin, -sin, cos)
+    tables[1, LANES:, LANES:] = np.where(is_sin, cos, sin)
+    tables[2], tables[3] = tables[0].T, tables[1].T
+    phase = 2.0 * np.pi * np.arange(HALF)[:, None] * np.arange(LANES)[None, :] / TOTAL
+    return tables.astype(jnp.bfloat16), np.concatenate([np.cos(phase), np.sin(phase)]).astype(np.float32)
 
 
 def times(value, c, s):
@@ -118,9 +111,9 @@
 
 
 def kernel(
-    pix, chan, sky_ref, flags_ref, modes_ref, block_ref, offset_ref, weight_ref, table_ref,
+    pix, chan, sky_ref, flags_ref, modes_ref, block_ref, offset_ref, weight_ref, table_ref, twiddle_ref,
     out_ref, stack_ref,
-    lines, flags, modes_v, block_v, offset_v, weights, chosen_w, meta, meta_own, meta_smem, table, spec, back, cube, staged,
+    lines, flags, modes_v, block_v, offset_v, weights, chosen_w, meta, meta_own, meta_smem, table, twiddle, spec, kept, back, cube, staged,
     part, sums, part2, sums2, flag_f, mask_ref, local_sem, out_sem, line_send, line_recv, flag_send, flag_recv,
     w_send, w_recv, m_send, m_recv, s_send, s_recv, t_send, t_recv,
 ):
@@ -145,6 +138,7 @@
         pltpu.make_async_copy(flags_ref, flags.at[me_c], local_sem.at[2]),
         pltpu.make_async_copy(weight_ref, weights.at[me_p], local_sem.at[3]),
         pltpu.make_async_copy(modes_ref, modes_v, local_sem.at[5]),
+        pltpu.make_async_copy(twiddle_ref, twiddle, local_sem.at[8]),
     ]
     places = [
         pltpu.make_async_copy(block_ref, block_v, local_sem.at[6]),
@@ -196,12 +190,64 @@
             lax.broadcasted_iota(jnp.int32, (32, LANES), 1) == lax.broadcasted_iota(jnp.int32, (32, LANES), 0) + 32 * q
         ).astype(jnp.float32)
         mask = mask + jnp.dot(turned[32 * q : 32 * q + 32], place, preferred_element_type=jnp.float32)
-    mask_ref[...] = mask
+    for k in range(HALF):
+        other = HALF if k == 0 else SLABS - k
+        gain = 1.0 if k == 0 else 0.5
+        mask_ref[k : k + 1, :LANES] = mask[k : k + 1] * gain
+        mask_ref[k : k + 1, LANES:] = mask[other : other + 1] * gain
 
     for copy in flag_copies:
         copy.wait()
     for c in range(chan):
         flag_f[c * per : (c + 1) * per, :] = flags[c].astype(jnp.float32)
+
+    def slab(n1, at):
+        c, s = n1 // per, n1 % per
+        value = lines[c, pl.ds(at, CHUNK), s * LANES : (s + 1) * LANES].astype(jnp.float32)
+        return value * flag_f[n1 : n1 + 1, :]
+
+    def filter_rows(step, carry):
+        for i, c in enumerate(chan_peers):
+            line_copy(i, c, step).wait_recv()
+        for j in range(STEP // CHUNK):
+            at = pl.multiple_of(step * STEP + j * CHUNK, CHUNK)
+            r = slice(j * CHUNK, (j + 1) * CHUNK)
+            y = real_forward([slab(n1, at) for n1 in range(SLABS)])
+            spec[0, r, :LANES] = y[0][0].astype(jnp.bfloat16)
+            spec[0, r, LANES:] = y[HALF][0].astype(jnp.bfloat16)
+            for k in range(1, HALF):
+                (re, im), cos, sin = y[k], twiddle[k : k + 1], twiddle[HALF + k : HALF + k + 1]
+                spec[k, r, :LANES] = (re * cos + im * sin).astype(jnp.bfloat16)
+                spec[k, r, LANES:] = (im * cos - re * sin).astype(jnp.bfloat16)
+        def stretch(ref, lo, hi):
+            return ref[lo:hi].reshape((hi - lo) * STEP, 2 * LANES)
+
+        for which, lo, hi in ((0, 0, 1), (1, 1, HALF)):
+            coeffs = jnp.dot(stretch(spec, lo, hi), table[which], preferred_element_type=jnp.float32)
+            for k in range(lo, hi):
+                mine = coeffs[(k - lo) * STEP : (k - lo + 1) * STEP]
+                kept[k] = (mine * mask_ref[k : k + 1]).astype(jnp.bfloat16)
+            ripple = jnp.dot(stretch(kept, lo, hi), table[2 + which], preferred_element_type=jnp.float32)
+            back[lo:hi] = ripple.reshape(hi - lo, STEP, 2 * LANES)
+        for j in range(STEP // CHUNK):
+            at = pl.multiple_of(step * STEP + j * CHUNK, CHUNK)
+            r = slice(j * CHUNK, (j + 1) * CHUNK)
+            z = [(back[0, r, :LANES], None)]
+            for k in range(1, HALF):
+                re, im = back[k, r, :LANES], back[k, r, LANES:]
+                cos, sin = twiddle[k : k + 1], twiddle[HALF + k : HALF + k + 1]
+                z.append((re * cos - im * sin, re * sin + im * cos))
+            z += [(back[0, r, LANES:], None)]
+            ripple = real_inverse(z)
+            for n1 in range(SLABS):
+                value = (slab(n1, at) - ripple[n1]).astype(jnp.bfloat16)
+                staged[pl.ds(at, CHUNK), n1 * LANES : (n1 + 1) * LANES] = value
+                cube[(step * (STEP // CHUNK) + j) * SLABS + n1] = value.astype(jnp.float32)
+        here = pl.ds(pl.multiple_of(step * STEP, STEP), STEP)
+        pltpu.make_async_copy(staged.at[here], out_ref.at[here], out_sem.at[step]).start()
+        return carry
+
+    lax.fori_loop(0, steps - 1, filter_rows, 0)
 
     meta[me_p] = meta_own[...]
     for copy in m_copies:
@@ -232,46 +278,7 @@
 
     power = lax.fori_loop(0, pix, choose, jnp.zeros((patch, LANES), jnp.float32))
 
-    def slab(n1, at):
-        c, s = n1 // per, n1 % per
-        value = lines[c, pl.ds(at, CHUNK), s * LANES : (s + 1) * LANES].astype(jnp.float32)
-        return value * flag_f[n1 : n1 + 1, :]
-
-    def filter_rows(step, carry):
-        for i, c in enumerate(chan_peers):
-            line_copy(i, c, step).wait_recv()
-        for j in range(STEP // CHUNK):
-            at = pl.multiple_of(step * STEP + j * CHUNK, CHUNK)
-            r = slice(j * CHUNK, (j + 1) * CHUNK)
-            y = real_forward([slab(n1, at) for n1 in range(SLABS)])
-            spec[0, r, :LANES] = y[0][0].astype(jnp.bfloat16)
-            spec[0, r, LANES:] = y[HALF][0].astype(jnp.bfloat16)
-            for k in range(1, HALF):
-                spec[k, r, :LANES] = y[k][0].astype(jnp.bfloat16)
-                spec[k, r, LANES:] = y[k][1].astype(jnp.bfloat16)
-        for k in range(HALF):
-            other = HALF if k == 0 else SLABS - k
-            gain = 1.0 if k == 0 else 0.5
-            chosen = jnp.concatenate([mask_ref[k : k + 1], mask_ref[other : other + 1]], axis=1) * gain
-            coeffs = jnp.dot(spec[k], table[k], preferred_element_type=jnp.float32)
-            kept = (coeffs * chosen).astype(jnp.bfloat16)
-            back[k] = lax.dot_general(kept, table[k], (((1,), (1,)), ((), ())), preferred_element_type=jnp.float32)
-        for j in range(STEP // CHUNK):
-            at = pl.multiple_of(step * STEP + j * CHUNK, CHUNK)
-            r = slice(j * CHUNK, (j + 1) * CHUNK)
-            z = [(back[0, r, :LANES], None)]
-            z += [(back[k, r, :LANES], back[k, r, LANES:]) for k in range(1, HALF)]
-            z += [(back[0, r, LANES:], None)]
-            ripple = real_inverse(z)
-            for n1 in range(SLABS):
-                value = (slab(n1, at) - ripple[n1]).astype(jnp.bfloat16)
-                staged[pl.ds(at, CHUNK), n1 * LANES : (n1 + 1) * LANES] = value
-                cube[(step * (STEP // CHUNK) + j) * SLABS + n1] = value.astype(jnp.float32)
-        here = pl.ds(pl.multiple_of(step * STEP, STEP), STEP)
-        pltpu.make_async_copy(staged.at[here], out_ref.at[here], out_sem.at[step]).start()
-        return carry
-
-    lax.fori_loop(0, steps, filter_rows, 0)
+    filter_rows(steps - 1, 0)
 
     lane = lax.broadcasted_iota(jnp.int32, (patch, LANES), 1)
 
@@ -332,7 +339,7 @@
         any_spec = pl.BlockSpec(memory_space=pl.ANY)
         vmem_spec = pl.BlockSpec(memory_space=pltpu.VMEM)
         dma = pltpu.SemaphoreType.DMA
-        table = jnp.asarray(mode_table())
+        table, twiddle = (jnp.asarray(v) for v in mode_tables())
         shapes = (
             jax.ShapeDtypeStruct((rows, TOTAL), jnp.bfloat16),
             jax.ShapeDtypeStruct((patch, LANES), jnp.float32),
@@ -340,7 +347,7 @@
         filtered, stack = pl.pallas_call(
             functools.partial(kernel, pix, chan),
             out_shape=shapes,
-            in_specs=[pl.BlockSpec(memory_space=pltpu.HBM)] * 7,
+            in_specs=[pl.BlockSpec(memory_space=pltpu.HBM)] * 8,
             out_specs=(any_spec, vmem_spec),
             scratch_shapes=[
                 pltpu.VMEM((chan, rows, width), jnp.bfloat16),
@@ -353,7 +360,9 @@
                 pltpu.VMEM((pix, 8, LANES), jnp.int32),
                 pltpu.VMEM((8, LANES), jnp.int32),
                 pltpu.SMEM((pix, 8, LANES), jnp.int32),
-                pltpu.VMEM((HALF, 2 * LANES, 2 * LANES), jnp.bfloat16),
+                pltpu.VMEM((4, 2 * LANES, 2 * LANES), jnp.bfloat16),
+                pltpu.VMEM((SLABS, LANES), jnp.float32),
+                pltpu.VMEM((HALF, STEP, 2 * LANES), jnp.bfloat16),
                 pltpu.VMEM((HALF, STEP, 2 * LANES), jnp.bfloat16),
                 pltpu.VMEM((HALF, STEP, 2 * LANES), jnp.float32),
                 pltpu.VMEM((rows // patch * SLABS, patch, LANES), jnp.float32),
@@ -363,8 +372,8 @@
                 pltpu.VMEM((patch, LANES), jnp.float32),
                 pltpu.VMEM((chan, patch, LANES), jnp.float32),
                 pltpu.VMEM((SLABS, LANES), jnp.float32),
-                pltpu.VMEM((SLABS, LANES), jnp.float32),
-                dma((8,)), dma((rows // STEP,)),
+                pltpu.VMEM((HALF, 2 * LANES), jnp.float32),
+                dma((9,)), dma((rows // STEP,)),
                 dma((rows // STEP, chan - 1)), dma((rows // STEP, chan - 1)), dma((chan - 1,)), dma((chan - 1,)),
                 dma((pix - 1,)), dma((pix - 1,)), dma((pix - 1,)), dma((pix - 1,)),
                 dma((pix - 1,)), dma((pix - 1,)),
@@ -374,7 +383,7 @@
         )(
             *(pltpu.with_memory_space_constraint(v, pltpu.HBM) for v in (
             sky_map, channel_flags.reshape(per, LANES), ripple_modes.reshape(32, LANES),
-            galaxy_block.reshape(1, count), galaxy_offset.reshape(1, count), galaxy_weight, table,
+            galaxy_block.reshape(1, count), galaxy_offset.reshape(1, count), galaxy_weight, table, twiddle,
             ))
         )
         return pl.pallas_call(

time: 33.3 us -> 33.4 us (level)
  no operation moved by 1% of the time
where the time goes in v3:
time: 33.4 us; the launch traced here: 33.3 us
  Pallas kernels  32.6 us (98%)
  between operations  0.64 us (2%)
    pallas_call x1, Pallas kernels, body(): pl.pallas_call(functools.partial(kernel, pix, chan), out_shape=shapes, in...  31.2 us
    pallas_call x1, Pallas kernels, body(): pl.pallas_call(hand_over, out_shape=shapes, in_specs=[any_spec, vmem_spec...  1.4 us

profile of v3, /device:TPU:0, one launch (start us, length us, event | category | flops | bytes accessed | tf_op | source)
XLA Modules:
  0.0 33.3 jit_solution(11113524658753999294)
XLA Ops:
  0.6 31.2 %shard_map.95 = (bf16[64,4096]{1,0:T(8,128)(2,1)S(1)}, f32[16,128]{1,0:T(8,128)S(1)}) custom-call(bf16[256,1024]{1,0:T(8,128)(2,1)} %sky_ref.1, s32[8,128]{1,0:T(8,128)} %bitcast.5, s32[32,128]{1,0:T(8,128)} %bitcast.4, s32[1,16]{1,0:T(1,128)} %bitcast.6, s32[1,16]{1,0:T(1,128)} %bitcast.7, bf16[16,16,128]{2,1,0:T(8,128)(2,1)} %weight_ref.1, ...), custom_call_target="tpu_custom_call" | custom-call | tf_op jit(solution)/shard_map/pallas_call | solution.py:347
  31.9 1.4 %shard_map.96 = (bf16[64,4096]{1,0:T(8,128)(2,1)}, f32[16,128]{1,0:T(8,128)}) custom-call(bf16[64,4096]{1,0:T(8,128)(2,1)S(1)} %get-tuple-element.4.filtered_ref, f32[16,128]{1,0:T(8,128)S(1)} %get-tuple-element.5.stack_ref), custom_call_target="tpu_custom_call" | custom-call | tf_op jit(solution)/shard_map/pallas_call | solution.py:389

commit v4 on v3

--- a/solution.py
+++ b/solution.py
@@ -15,7 +15,7 @@
 TOTAL = LANES * SLABS
 HALF = SLABS // 2
 CHUNK = 16
-STEP = 16
+STEP = 64
 
 
 def mode_tables():
@@ -110,6 +110,20 @@
     return out
 
 
+def partners(me, size):
+    if size & (size - 1):
+        return [lax.rem(me + d, size) for d in range(1, size)]
+    found = []
+    for d in range(size - 1, 0, -1):
+        at, bit = me, 1
+        while bit < size:
+            if d & bit:
+                at = at + bit * (1 - 2 * lax.rem(lax.div(at, bit), 2))
+            bit *= 2
+        found.append(at)
+    return found
+
+
 def kernel(
     pix, chan, sky_ref, flags_ref, modes_ref, block_ref, offset_ref, weight_ref, table_ref, twiddle_ref,
     out_ref, stack_ref,
@@ -125,8 +139,8 @@
     steps = rows // STEP
 
     barrier = pltpu.get_barrier_semaphore()
-    chan_peers = [lax.rem(me_c + d, chan) for d in range(1, chan)]
-    pix_peers = [lax.rem(me_p + d, pix) for d in range(1, pix)]
+    chan_peers = partners(me_c, chan)
+    pix_peers = partners(me_p, pix)
     for c in chan_peers:
         pl.semaphore_signal(barrier, inc=1, device_id=(me_p, c), device_id_type=MESH)
     for p in pix_peers:
@@ -271,6 +285,7 @@
             meta_smem[p, 2, g] = safe * SLABS + base
             meta_smem[p, 3, g] = safe * SLABS + jnp.minimum(base + 1, SLABS - 1)
             meta_smem[p, 4, g] = shift
+            meta_smem[p, 5, g] = lax.rem(LANES - shift, LANES)
             w = weights[p, g].astype(jnp.float32)
             acc = acc + w * w
             chosen_w[p, g] = jnp.where(local == safe, w, 0.0)
@@ -288,7 +303,7 @@
             high = cube[meta_smem[p, 3, g]]
             shift = meta_smem[p, 4, g]
             joined = jnp.where(lane >= shift, low, high)
-            panel = pltpu.roll(joined, lax.rem(LANES - shift, LANES), 1)
+            panel = pltpu.roll(joined, meta_smem[p, 5, g], 1)
             acc = acc + chosen_w[p, g] * panel
         return acc
 

time: 33.4 us -> 32.2 us (0.964)
  Pallas kernels: 32.6 us -> 31.4 us
    pallas_call x1, Pallas kernels: 31.2 us -> 30 us  [body(): pl.pallas_call(functools.partial(kernel, pix, chan), out_shape=shapes, in...]
where the time goes in v4:
time: 32.2 us; the launch traced here: 32 us
  Pallas kernels  31.4 us (98%)
  between operations  0.64 us (2%)
    pallas_call x1, Pallas kernels, body(): pl.pallas_call(functools.partial(kernel, pix, chan), out_shape=shapes, in...  30 us
    pallas_call x1, Pallas kernels, body(): pl.pallas_call(hand_over, out_shape=shapes, in_specs=[any_spec, vmem_spec...  1.4 us

profile of v4, /device:TPU:0, one launch (start us, length us, event | category | flops | bytes accessed | tf_op | source)
XLA Modules:
  0.0 32.0 jit_solution(16868527424414826850)
XLA Ops:
  0.6 30.0 %shard_map.95 = (bf16[64,4096]{1,0:T(8,128)(2,1)S(1)}, f32[16,128]{1,0:T(8,128)S(1)}) custom-call(bf16[256,1024]{1,0:T(8,128)(2,1)} %sky_ref.1, s32[8,128]{1,0:T(8,128)} %bitcast.5, s32[32,128]{1,0:T(8,128)} %bitcast.4, s32[1,16]{1,0:T(1,128)} %bitcast.6, s32[1,16]{1,0:T(1,128)} %bitcast.7, bf16[16,16,128]{2,1,0:T(8,128)(2,1)} %weight_ref.1, ...), custom_call_target="tpu_custom_call" | custom-call | tf_op jit(solution)/shard_map/pallas_call | solution.py:362
  30.6 1.4 %shard_map.96 = (bf16[64,4096]{1,0:T(8,128)(2,1)}, f32[16,128]{1,0:T(8,128)}) custom-call(bf16[64,4096]{1,0:T(8,128)(2,1)S(1)} %get-tuple-element.4.filtered_ref, f32[16,128]{1,0:T(8,128)S(1)} %get-tuple-element.5.stack_ref), custom_call_target="tpu_custom_call" | custom-call | tf_op jit(solution)/shard_map/pallas_call | solution.py:404
